TPU v7x, 32 devices: a whole 2x2x4 slice. The times are simulated.
32 devices in a mesh: groups: 2 (over x), branch: 2 (over core), sub: 8 (over z, y).
Axes of the slice: x: 2, y: 2, z: 4, core: 2. Of those that a mesh axis runs over, the one named last changes fastest.
Arguments:
- dispatch: float32 [128, 168, 2048], P(('groups', 'branch', 'sub')), parts along dimension 0, may hold values from 0 to 3
- multiplier: float32 [128, 48, 2048], P(('groups', 'branch', 'sub')), parts along dimension 0, may hold values from -3 to 3
- node_of: int32 [128], P(('groups', 'branch', 'sub')), parts along dimension 0, may hold values from 0 to 7, as said below
- prob_weight: int32 [128], P(('groups', 'branch', 'sub')), parts along dimension 0, may hold values from 1 to 16
- commitment: int32 [128, 168, 2048], P(('groups', 'branch', 'sub')), parts along dimension 0, may hold values 0 or 1
- zone_of: int32 [2048], replicated, may hold values from 0 to 31
- capacity: float32 [2048], replicated, may hold values from 0.5 to 4
- linear_cost: float32 [2048], replicated, may hold values from -0.5 to 1
- quad_cost: float32 [2048], replicated, may hold values from 0.5 to 2
- demand: float32 [128, 168, 32], P(('groups', 'branch', 'sub')), parts along dimension 0, may hold values from 19 to 64
Outputs:
- new_dispatch: float32 [128, 168, 2048], P(('groups', 'branch', 'sub')), parts along dimension 0
- new_multiplier: float32 [128, 48, 2048], P(('groups', 'branch', 'sub')), parts along dimension 0
- next_average: float32 [128, 48, 2048], P(('groups', 'branch', 'sub')), parts along dimension 0
- deviation: float32 [2], P('groups'), parts along dimension 0
There are 2 independent parts, one for each index of `groups`. A program takes and returns all parts, laid end to end along the dimension named above; an argument that names none is the same for every part. Nothing has to cross between parts.
Inputs may be any that keep to these rules, and one draw needn't show every extreme that they name: `node_of`: within each aligned block of 32 scenarios (one day-one branch), every node number holds exactly 4 scenarios.
All inputs are finite; a program needn't handle non-finite values. No bound on the sum of `commitment` on one device may be relied on, other than what follows from the above.
Results may differ from a plain program's by a relative error of at most 0.0001.
Values sent between devices are 32-bit elements; how exact they have to be, the bound alone decides.
A program may use at most 128 MiB of HBM per device.

v0:
```python
import jax
import jax.numpy as jnp
from jax import lax
from jax.sharding import PartitionSpec as P

DAY = 24
NODES_BR = 8
STEPS = 3
rho_value = 1.0
step_size = 0.3


def average(early_part, prob_weight, node_of, riding):
    weighting = prob_weight.astype(jnp.float32)
    scen_local = early_part.shape[0]
    gens = early_part.shape[2]
    member = (node_of[None, :] == jnp.arange(NODES_BR, dtype=jnp.int32)[:, None]).astype(
        jnp.float32
    )
    weighted = member * weighting[None, :]
    day_one = jnp.einsum(
        "s,stg->tg", weighting, early_part[:, :DAY], precision=lax.Precision.HIGHEST
    )
    weight_sum = jnp.sum(weighting)[None]
    day_two = jnp.einsum(
        "ks,stg->ktg", weighted, early_part[:, DAY:], precision=lax.Precision.HIGHEST
    )
    node_weight = jnp.sum(weighted, axis=1)
    day_two, node_weight = lax.psum((day_two, node_weight), "sub")
    day_one, weight_sum, riding = lax.psum((day_one, weight_sum, riding), ("branch", "sub"))
    root_mean = day_one / weight_sum[0]
    node_mean = day_two / node_weight[:, None, None]
    assigned = jnp.einsum("ks,ktg->stg", member, node_mean, precision=lax.Precision.HIGHEST)
    spread_root = jnp.broadcast_to(root_mean[None], (scen_local, DAY, gens))
    return (jnp.concatenate([spread_root, assigned], axis=1), weight_sum, riding)


def shards(
    dispatch,
    multiplier,
    node_of,
    prob_weight,
    commitment,
    zone_of,
    capacity,
    linear_cost,
    quad_cost,
    demand,
):
    section_hours = multiplier.shape[1]
    gens = zone_of.shape[0]
    zones_count = demand.shape[2]
    weighting = prob_weight.astype(jnp.float32)
    nothing = jnp.zeros((1,), jnp.float32)
    averages, weight_sum, unused = average(
        dispatch[:, :section_hours], prob_weight, node_of, nothing
    )
    spread_gap = dispatch[:, :section_hours] - averages
    local_spread = jnp.sum(weighting[:, None, None] * spread_gap * spread_gap)[None]
    dev_total = lax.psum(local_spread, ("branch", "sub"))
    new_multiplier = multiplier + rho_value * spread_gap
    zone_table = (zone_of[:, None] == jnp.arange(zones_count, dtype=jnp.int32)[None, :]).astype(
        jnp.float32
    )
    ceiling = capacity[None, None, :] * commitment.astype(jnp.float32)
    balance = zones_count / gens
    current = dispatch
    for sweep in range(STEPS):
        zone_sum = jnp.einsum("stg,gz->stz", current, zone_table, precision=lax.Precision.HIGHEST)
        mismatch = zone_sum - demand
        feedback = jnp.einsum("stz,gz->stg", mismatch, zone_table, precision=lax.Precision.HIGHEST)
        gradient = linear_cost + quad_cost * current + balance * feedback
        hedged = (
            gradient[:, :section_hours]
            + new_multiplier
            + rho_value * (current[:, :section_hours] - averages)
        )
        gradient = jnp.concatenate([hedged, gradient[:, section_hours:]], axis=1)
        current = jnp.clip(current - step_size * gradient, 0.0, ceiling)
    next_average, unused_sum, carried = average(
        current[:, :section_hours], prob_weight, node_of, nothing
    )
    deviation = dev_total / (weight_sum * section_hours * gens)
    return (current, new_multiplier, next_average, deviation)


def solution(mesh):
    in_specs = (
        P(("groups", "branch", "sub"), None, None),
        P(("groups", "branch", "sub"), None, None),
        P(("groups", "branch", "sub")),
        P(("groups", "branch", "sub")),
        P(("groups", "branch", "sub"), None, None),
        P(),
        P(),
        P(),
        P(),
        P(("groups", "branch", "sub"), None, None),
    )
    out_specs = (
        P(("groups", "branch", "sub"), None, None),
        P(("groups", "branch", "sub"), None, None),
        P(("groups", "branch", "sub"), None, None),
        P("groups"),
    )
    return jax.shard_map(shards, mesh=mesh, in_specs=in_specs, out_specs=out_specs, check_vma=False)
```

profile of v0, /device:TPU:0, one launch (start us, length us, event | category | flops | bytes accessed | tf_op | source)
XLA Modules:
  0.0 428.4 jit_solution(12756518674870253161)
XLA Ops:
  7.3 1.5 fusion.62
  8.8 2.5 fusion.25
  11.3 0.7 copy.33
  12.0 0.0 all-reduce.7.cloned.1.call-start
  12.1 0.7 convert_element_type.5
  12.7 4.0 fusion.23
  16.8 0.6 convert_reduce_fusion
  17.4 0.1 select_reduce_fusion
  17.5 35.9 %psum.56 = f32[1]{0:T(128)} all-reduce(f32[1]{0:T(128)} %bitcast.4), channel_id=1, replica_groups=mesh['groups'=2,'branch'=2,'sub'=8] {'branch','sub'}, use_global_device_ids=true, to_apply=%region_2.0 | all-reduce | flops 1 | bytes 8 | tf_op jit(solution)/shard_map/psum | solution.py:30
  53.4 17.6 %psum.58 = f32[8]{0:T(128)S(1)} all-reduce(f32[8]{0:T(128)S(1)} %select_reduce_fusion), channel_id=1, replica_groups=mesh['groups'=2,'branch'=2,'sub'=8] {'sub'}, use_global_device_ids=true, to_apply=%region_5.0 | all-reduce | flops 8 | bytes 64 | tf_op jit(solution)/shard_map/psum | solution.py:29
  71.1 5.7 %fusion.18 = f32[4,168,32]{1,2,0:T(8,128)S(1)} fusion(f32[4,168,32]{1,2,0:T(8,128)S(1)} %copy-done.6, f32[4,168,2048]{2,1,0:T(8,128)} %param.10, s32[2048]{0:T(1024)S(1)} %copy-done.7), kind=kOutput, calls=%fused_computation.36 | convolution fusion | flops 528569344 | bytes 5685248 | tf_op jit(solution)/shard_map/stg,gz->stz/dot_general | solution.py:69
  76.8 3.0 multiply_add_fusion.2
  79.8 2.4 copy-done.1
  82.2 22.3 %all-reduce.5.cloned.1.call-done = f32[24,2048]{1,0:T(8,128)} async-done(((f32[24,2048]{1,0:T(8,128)}), f32[24,2048]{1,0:T(8,128)}) %all-reduce.5.cloned.1.call-update) | async-done | bytes 196624 | tf_op jit(solution)/shard_map/psum | solution.py:30
  104.5 1.6 broadcast_divide_fusion.1
  106.1 90.5 %all-reduce.7.cloned.1.call-done = f32[8,24,2048]{2,0,1:T(8,128)} async-done(((f32[8,24,2048]{2,0,1:T(8,128)}), f32[8,24,2048]{2,0,1:T(8,128)}) %all-reduce.7.cloned.1.call-update) | async-done | bytes 1572880 | tf_op jit(solution)/shard_map/psum | solution.py:29
  196.5 2.5 fusion.16
  199.0 0.5 copy.14
  199.6 0.1 broadcast_in_dim.9
  199.7 2.9 fusion.12
  202.5 0.8 slice-done.4
  203.3 0.7 slice-done.1
  204.0 4.0 fusion.2
  208.0 3.0 convolution_subtract_fusion.1
  211.0 3.0 multiply_add_fusion.1
  214.1 0.4 slice.63
  214.5 0.5 fusion.11
  215.1 1.2 slice-done.2
  216.2 0.5 slice-done.3
  216.7 2.9 fusion.5
  219.6 3.0 convolution_subtract_fusion
  222.6 3.0 multiply_add_fusion
  225.6 0.5 fusion.10
  226.2 0.3 slice.66
  226.4 2.6 fusion.8
  229.1 2.4 copy-done.4
  231.5 0.1 fusion.61
  231.6 1.9 fusion.21
  233.5 0.7 copy.32
  234.3 3.3 fusion.19
  238.3 32.6 %psum.61 = f32[1]{0:T(128)} all-reduce(f32[1]{0:T(128)} %bitcast.10), channel_id=1, replica_groups=mesh['groups'=2,'branch'=2,'sub'=8] {'branch','sub'}, use_global_device_ids=true, to_apply=%region_9.10 | all-reduce | flops 1 | bytes 8 | tf_op jit(solution)/shard_map/psum | solution.py:60
  271.5 52.0 %all-reduce.9.cloned.1.call-done = f32[24,2048]{1,0:T(8,128)} async-done(((f32[24,2048]{1,0:T(8,128)}), f32[24,2048]{1,0:T(8,128)}) %all-reduce.9.cloned.1.call-update) | async-done | bytes 196624 | tf_op jit(solution)/shard_map/psum | solution.py:30
  323.6 1.6 broadcast_divide_fusion
  325.1 90.3 %all-reduce.11.cloned.1.call-done = f32[8,24,2048]{2,0,1:T(8,128)} async-done(((f32[8,24,2048]{2,0,1:T(8,128)}), f32[8,24,2048]{2,0,1:T(8,128)}) %all-reduce.11.cloned.1.call-update) | async-done | bytes 1572880 | tf_op jit(solution)/shard_map/psum | solution.py:29
  415.4 2.4 fusion.14
  417.8 0.2 broadcast_in_dim.10
  418.0 0.7 pad_maximum_fusion.1
  418.7 2.1 copy.15
  (39 shorter events, 0.3 us)
Async XLA Ops:
  7.2 9.6 %copy-start.11 = (s32[4]{0:T(128)S(1)}, s32[4]{0:T(128)}, u32[]{:S(2)}) copy-start(s32[4]{0:T(128)} %param.13) | copy-start | bytes 52
  7.2 10.2 %copy-start.12 = (s32[4]{0:T(128)S(1)}, s32[4]{0:T(128)}, u32[]{:S(2)}) copy-start(s32[4]{0:T(128)} %param.12) | copy-start | bytes 52
  7.2 63.9 %copy-start.7 = (s32[2048]{0:T(1024)S(1)}, s32[2048]{0:T(1024)}, u32[]{:S(2)}) copy-start(s32[2048]{0:T(1024)} %param.15) | copy-start | bytes 24580
  7.2 63.8 %copy-start.6 = (f32[4,168,32]{1,2,0:T(8,128)S(1)}, f32[4,168,32]{1,2,0:T(8,128)}, u32[]{:S(2)}) copy-start(f32[4,168,32]{1,2,0:T(8,128)} %param.19) | copy-start | bytes 258052
  7.2 97.3 %all-reduce.5.cloned.1.call-start = ((), (), s32[]{:S(2)}) async-start(), calls=%async_computation | async-start | bytes 393216 | tf_op jit(solution)/shard_map/psum | solution.py:30
  8.8 68.0 %copy-start.9 = (f32[2048]{0:T(1024)S(1)}, f32[2048]{0:T(1024)}, u32[]{:S(2)}) copy-start(f32[2048]{0:T(1024)} %param.18) | copy-start | bytes 24580
  8.8 68.0 %copy-start.10 = (f32[2048]{0:T(1024)S(1)}, f32[2048]{0:T(1024)}, u32[]{:S(2)}) copy-start(f32[2048]{0:T(1024)} %param.17) | copy-start | bytes 24580
  12.0 184.5 %all-reduce.7.cloned.1.call-start = ((), (), s32[]{:S(2)}) async-start(), calls=%async_computation.1 | async-start | bytes 3145728 | tf_op jit(solution)/shard_map/psum | solution.py:29
  16.7 306.8 %all-reduce.9.cloned.1.call-start = ((), (), s32[]{:S(2)}) async-start(), calls=%async_computation.2 | async-start | bytes 393216 | tf_op jit(solution)/shard_map/psum | solution.py:30
  71.0 5.7 %copy-start = (f32[4,168,2048]{2,1,0:T(8,128)S(1)}, f32[4,168,2048]{2,1,0:T(8,128)}, u32[]{:S(2)}) copy-start(f32[4,168,2048]{2,1,0:T(8,128)} %param.10) | copy-start | bytes 16515076
  79.8 2.4 copy-start.1
  82.2 117.4 %copy-start.5 = (f32[4,48,2048]{2,1,0:T(8,128)S(1)}, f32[4,48,2048]{2,1,0:T(8,128)}, u32[]{:S(2)}) copy-start(f32[4,48,2048]{2,1,0:T(8,128)} %param.11) | copy-start | bytes 4718596
  196.5 3.1 copy-start.2
  199.5 3.0 slice-start
  199.5 3.8 slice-start.4
  199.5 3.8 copy-start.8
  199.6 4.4 %slice-start.1 = ((s8[5505024]{0:T(1024)(128)(4,1)}), s8[1310720]{0:T(1024)(128)(4,1)S(1)}, s32[]{:S(2)}) async-start(s8[5505024]{0:T(1024)(128)(4,1)} %bitcast.41), calls=%async_computation.5 | async-start | bytes 2621440
  202.5 23.1 %copy-start.3 = (f32[4,48,2048]{2,1,0:T(8,128)}, f32[4,48,2048]{2,1,0:T(8,128)S(1)}, u32[]{:S(2)}) copy-start(f32[4,48,2048]{2,1,0:T(8,128)S(1)} %get-tuple-element.9) | copy-start | bytes 4718596
  214.0 2.2 slice-start.2
  214.5 2.2 slice-start.3
  229.1 2.4 copy-start.4
  234.3 181.1 %all-reduce.11.cloned.1.call-start = ((), (), s32[]{:S(2)}) async-start(), calls=%async_computation.3 | async-start | bytes 3145728 | tf_op jit(solution)/shard_map/psum | solution.py:29
Sparse Core Ops, SparseCore 0:
  12.1 92.3 all-reduce.4
  108.6 87.8 all-reduce.6
  234.4 89.0 all-reduce.8
  327.5 87.8 all-reduce.10
where the time goes:
time: 429 us; the launch traced here: 428 us
  waiting for transfers between devices  255 us (59%)
  blocking collectives  86.1 us (20%)
  matrix products  37.2 us (9%)
  other arithmetic  18.6 us (4%)
  between operations  16.5 us (4%)
  local copies, waits for them, and re-layouts  14.7 us (3%)
    psum x2, waiting for transfers between devices, average(): day_two, node_weight = lax.psum((day_two, node_weight), 'sub')  181 us
    psum x2, waiting for transfers between devices, average(): lax.psum((day_one, weight_sum, riding), ('branch', 'sub'))  74.3 us
    psum x1, blocking collectives, average(): lax.psum((day_one, weight_sum, riding), ('branch', 'sub'))  35.9 us
    psum x1, blocking collectives, shards(): dev_total = lax.psum(local_spread, ('branch', 'sub'))  32.6 us
    psum x1, blocking collectives, average(): day_two, node_weight = lax.psum((day_two, node_weight), 'sub')  17.6 us
    dot_general x3, matrix products, shards(): jnp.einsum('stg,gz->stz', current, zone_table, precision=lax.Precision.HI...  11.6 us
    min x3, other arithmetic, shards(): current = jnp.clip(current - step_size * gradient, 0.0, ceiling)  9.51 us
    unnamed x35, local copies, waits for them, and re-layouts  9.42 us
  transfers between devices with their start and end apart: 4, of which 4 were waited for; matrix products, arithmetic and copies ran while one was open for 5% of the time, Pallas kernels for 0%

commit v1 on v0

--- a/solution.py
+++ b/solution.py
@@ -27,7 +27,7 @@
     )
     node_weight = jnp.sum(weighted, axis=1)
     day_two, node_weight = lax.psum((day_two, node_weight), "sub")
-    day_one, weight_sum, riding = lax.psum((day_one, weight_sum, riding), ("branch", "sub"))
+    day_one, weight_sum, riding = lax.psum(lax.psum((day_one, weight_sum, riding), "sub"), "branch")
     root_mean = day_one / weight_sum[0]
     node_mean = day_two / node_weight[:, None, None]
     assigned = jnp.einsum("ks,ktg->stg", member, node_mean, precision=lax.Precision.HIGHEST)

time: 429 us -> 302 us (0.70)
  waiting for transfers between devices: 255 us -> 147 us
  blocking collectives: 86.1 us -> 63.8 us
    psum x2, waiting for transfers between devices: 181 us -> 113 us  [average(): day_two, node_weight = lax.psum((day_two, node_weight), 'sub')]
    psum x2, waiting for transfers between devices: 74.3 us -> 33.6 us  [average(): lax.psum(lax.psum((day_one, weight_sum, riding), 'sub'), 'branch')]
    psum x1, blocking collectives: 35.9 us -> 3.13 us  [average(): lax.psum(lax.psum((day_one, weight_sum, riding), 'sub'), 'branch')]
    psum x1, blocking collectives: 17.6 us -> 24.7 us  [average(): day_two, node_weight = lax.psum((day_two, node_weight), 'sub')]
    unnamed x35 -> x31, local copies, waits for them, and re-layouts: 9.42 us -> 9.04 us
  transfers between devices with their start and end apart: 4 -> 4, of which waited for: 4 -> 4; matrix products, arithmetic and copies ran while one was open for 5% -> 6% of each run, Pallas kernels for 0% -> 0%
where the time goes in v1:
time: 302 us
  waiting for transfers between devices  147 us (49%)
  blocking collectives  63.8 us (21%)
  matrix products  39.5 us (13%)
  other arithmetic  20.3 us (7%)
  between operations  16.5 us (5%)
  local copies, waits for them, and re-layouts  14.4 us (5%)
    psum x2, waiting for transfers between devices, average(): day_two, node_weight = lax.psum((day_two, node_weight), 'sub')  113 us
    psum x1, blocking collectives, shards(): dev_total = lax.psum(local_spread, ('branch', 'sub'))  36 us
    psum x2, waiting for transfers between devices, average(): lax.psum(lax.psum((day_one, weight_sum, riding), 'sub'), 'branch')  33.6 us
    psum x1, blocking collectives, average(): day_two, node_weight = lax.psum((day_two, node_weight), 'sub')  24.7 us
    dot_general x3, matrix products, shards(): jnp.einsum('stg,gz->stz', current, zone_table, precision=lax.Precision.HI...  11.5 us
    dot_general x3, matrix products, shards(): jnp.einsum('stz,gz->stg', mismatch, zone_table, precision=lax.Precision.H...  11.5 us
    min x3, other arithmetic, shards(): current = jnp.clip(current - step_size * gradient, 0.0, ceiling)  9.8 us
    unnamed x31, local copies, waits for them, and re-layouts  9.04 us
  transfers between devices with their start and end apart: 4, of which 4 were waited for; matrix products, arithmetic and copies ran while one was open for 6% of the time, Pallas kernels for 0%

profile of v1, /device:TPU:0, one launch (start us, length us, event | category | flops | bytes accessed | tf_op | source)
XLA Modules:
  0.0 301.8 jit_solution(16410130114054210034)
XLA Ops:
  7.3 0.7 convert_element_type.5
  7.9 1.5 fusion.62
  9.4 2.5 fusion.25
  11.9 0.7 copy.33
  12.6 4.0 %fusion.23 = f32[8,24,2048]{2,0,1:T(8,128)} fusion(f32[4,24,2048]{2,1,0:T(8,128)S(1)} %get-tuple-element.20, f32[4]{0:T(128)S(1)} %convert_element_type.5, s32[4]{0:T(128)} %param.12), kind=kOutput, calls=%fused_computation.41 | convolution fusion | flops 18874432 | bytes 2359328 | tf_op jit(solution)/shard_map/ks,stg->ktg/dot_general | solution.py:25
  16.7 0.0 all-reduce.8.cloned.1.call-start
  16.7 0.6 convert_reduce_fusion
  17.3 0.1 select_reduce_fusion
  17.4 24.7 %all-reduce = (f32[8]{0:T(128)S(1)}, f32[1]{0:T(128)}) all-reduce(f32[8]{0:T(128)S(1)} %select_reduce_fusion, f32[1]{0:T(128)} %bitcast.4), channel_id=1, replica_groups=mesh['groups'=2,'branch'=2,'sub'=8] {'sub'}, use_global_device_ids=true, to_apply=%region_7.0 | all-reduce | flops 9 | bytes 72 | tf_op jit(solution)/shard_map/psum | solution.py:29
  42.1 3.1 %psum.82 = f32[1]{0:T(128)} all-reduce(f32[1]{0:T(128)} %get-tuple-element.9), channel_id=1, replica_groups=mesh['groups'=2,'branch'=2,'sub'=8] {'branch'}, use_global_device_ids=true, to_apply=%region_4.0 | all-reduce | flops 1 | bytes 8 | tf_op jit(solution)/shard_map/psum | solution.py:30
  45.2 5.6 %fusion.18 = f32[4,168,32]{1,2,0:T(8,128)S(1)} fusion(f32[4,168,32]{1,2,0:T(8,128)S(1)} %copy-done.4, f32[4,168,2048]{2,1,0:T(8,128)} %param.10, s32[2048]{0:T(1024)S(1)} %copy-done.5), kind=kOutput, calls=%fused_computation.36 | convolution fusion | flops 528569344 | bytes 5685248 | tf_op jit(solution)/shard_map/stg,gz->stz/dot_general | solution.py:69
  50.8 5.6 %multiply_add_fusion.2 = f32[4,168,2048]{2,1,0:T(8,128)S(1)} fusion(f32[4,168,2048]{2,1,0:T(8,128)} %param.10, f32[4,168,32]{1,2,0:T(8,128)S(1)} %fusion.18, f32[2048]{0:T(1024)S(1)} %copy-done.7, f32[2048]{0:T(1024)S(1)} %copy-done.8, s32[2048]{0:T(1024)S(1)} %copy-done.5), kind=kOutput, calls=%fused_computation.14 | convolution fusion | flops 534052864 | bytes 11120640 | tf_op jit(solution)/shard_map/stz,gz->stg/dot_general | solution.py:71
  56.4 2.4 copy-done
  58.8 54.9 %all-reduce.14.cloned.1.call-done = (f32[8,24,2048]{2,0,1:T(8,128)}, f32[24,2048]{1,0:T(8,128)}) async-done(((f32[8,24,2048]{2,0,1:T(8,128)}, f32[24,2048]{1,0:T(8,128)}), (f32[8,24,2048]{2,0,1:T(8,128)}, f32[24,2048]{1,0:T(8,128)})) %all-reduce.14.cloned.1.call-update) | async-done | bytes 1769488 | tf_op jit(solution)/shard_map/psum | solution.py:29
  113.8 0.2 all-reduce.12.cloned.1.call-start
  114.0 2.4 fusion.16
  116.4 1.3 copy.14
  117.7 16.1 %all-reduce.8.cloned.1.call-done = f32[24,2048]{1,0:T(8,128)} async-done(((f32[24,2048]{1,0:T(8,128)}), f32[24,2048]{1,0:T(8,128)}) %all-reduce.8.cloned.1.call-update) | async-done | bytes 196624 | tf_op jit(solution)/shard_map/psum | solution.py:30
  133.8 1.9 broadcast_divide_fusion.1
  135.7 0.1 broadcast_in_dim.9
  135.8 4.1 %fusion.12 = (f32[4,48,2048]{2,1,0:T(8,128)S(1)}, f32[4,48,2048]{2,1,0:T(8,128)S(1)}, f32[]{:T(128)}) fusion(f32[4,168,2048]{2,1,0:T(8,128)} %copy-done, f32[4,24,2048]{2,1,0:T(8,128)} %copy.14, f32[4,24,2048]{2,1,0:T(8,128)S(1)} %broadcast_in_dim.9, f32[4,168,2048]{2,1,0:T(8,128)} %param.10, f32[4,48,2048]{2,1,0:T(8,128)} %param.11, ...), kind=kLoop, calls=%fused_computation.25 | loop fusion | flops 3145727 | bytes 9437204 | tf_op jit(solution)/shard_map/add | solution.py:74
  139.9 4.3 %fusion.2 = f32[4,168,2048]{2,1,0:T(8,128)S(1)} fusion(f32[4,168,2048]{2,1,0:T(8,128)S(1)} %bitcast.42, f32[4,120,2048]{2,1,0:T(8,128)S(1)} %slice-done.4, f32[4,48,2048]{2,1,0:T(8,128)S(1)} %get-tuple-element.14, s32[4,168,2048]{2,1,0:T(8,128)} %param.14, f32[2048]{0:T(1024)S(1)} %copy-done.6), kind=kLoop, calls=%fused_computation.3 | loop fusion | flops 9633792 | bytes 22028288 | tf_op jit(solution)/shard_map/jit(clip)/min | solution.py:79
  144.2 3.0 convolution_subtract_fusion.1
  147.2 3.0 multiply_add_fusion.1
  150.3 0.3 slice.63
  150.5 0.8 copy-done.2
  151.4 0.5 fusion.11
  151.9 0.8 slice-done.2
  152.7 0.4 slice-done.3
  153.1 2.8 fusion.5
  156.0 3.0 convolution_subtract_fusion
  159.0 3.0 multiply_add_fusion
  162.0 0.5 fusion.10
  162.5 0.4 slice.66
  163.0 2.6 fusion.8
  165.6 2.4 copy-done.3
  168.1 0.1 fusion.61
  168.2 1.9 fusion.21
  170.1 0.7 copy.32
  170.8 3.3 %fusion.19 = f32[8,24,2048]{2,0,1:T(8,128)} fusion(f32[4,24,2048]{2,1,0:T(8,128)S(1)} %get-tuple-element.18, f32[4]{0:T(128)S(1)} %convert_element_type.5, s32[4]{0:T(128)S(1)} %copy-done.10), kind=kOutput, calls=%fused_computation.37 | convolution fusion | flops 18874432 | bytes 2359328 | tf_op jit(solution)/shard_map/ks,stg->ktg/dot_general | solution.py:25
  174.8 36.0 %psum.88 = f32[1]{0:T(128)} all-reduce(f32[1]{0:T(128)} %bitcast.10), channel_id=1, replica_groups=mesh['groups'=2,'branch'=2,'sub'=8] {'branch','sub'}, use_global_device_ids=true, to_apply=%region_12.13 | all-reduce | flops 1 | bytes 8 | tf_op jit(solution)/shard_map/psum | solution.py:60
  211.5 58.4 %all-reduce.12.cloned.1.call-done = (f32[8,24,2048]{2,0,1:T(8,128)}, f32[24,2048]{1,0:T(8,128)}) async-done(((f32[8,24,2048]{2,0,1:T(8,128)}, f32[24,2048]{1,0:T(8,128)}), (f32[8,24,2048]{2,0,1:T(8,128)}, f32[24,2048]{1,0:T(8,128)})) %all-reduce.12.cloned.1.call-update) | async-done | bytes 1769488 | tf_op jit(solution)/shard_map/psum | solution.py:29
  269.9 2.4 fusion.14
  272.3 17.4 %all-reduce.10.cloned.1.call-done = f32[24,2048]{1,0:T(8,128)} async-done(((f32[24,2048]{1,0:T(8,128)}), f32[24,2048]{1,0:T(8,128)}) %all-reduce.10.cloned.1.call-update) | async-done | bytes 196624 | tf_op jit(solution)/shard_map/psum | solution.py:30
  289.7 1.6 broadcast_divide_fusion
  291.3 0.2 broadcast_in_dim.10
  291.5 0.5 pad_maximum_fusion.1
  292.1 2.1 copy.15
  (35 shorter events, 0.2 us)
Async XLA Ops:
  7.2 9.6 %copy-start.9 = (s32[4]{0:T(128)S(1)}, s32[4]{0:T(128)}, u32[]{:S(2)}) copy-start(s32[4]{0:T(128)} %param.13) | copy-start | bytes 52
  7.2 10.2 %copy-start.10 = (s32[4]{0:T(128)S(1)}, s32[4]{0:T(128)}, u32[]{:S(2)}) copy-start(s32[4]{0:T(128)} %param.12) | copy-start | bytes 52
  7.2 38.0 %copy-start.5 = (s32[2048]{0:T(1024)S(1)}, s32[2048]{0:T(1024)}, u32[]{:S(2)}) copy-start(s32[2048]{0:T(1024)} %param.15) | copy-start | bytes 24580
  7.2 38.0 %copy-start.4 = (f32[4,168,32]{1,2,0:T(8,128)S(1)}, f32[4,168,32]{1,2,0:T(8,128)}, u32[]{:S(2)}) copy-start(f32[4,168,32]{1,2,0:T(8,128)} %param.19) | copy-start | bytes 258052
  7.2 106.5 %all-reduce.14.cloned.1.call-start = ((), (), s32[]{:S(2)}) async-start(), calls=%async_computation.3 | async-start | bytes 3538944 | tf_op jit(solution)/shard_map/psum | solution.py:29
  9.4 41.4 %copy-start.7 = (f32[2048]{0:T(1024)S(1)}, f32[2048]{0:T(1024)}, u32[]{:S(2)}) copy-start(f32[2048]{0:T(1024)} %param.18) | copy-start | bytes 24580
  9.4 41.4 %copy-start.8 = (f32[2048]{0:T(1024)S(1)}, f32[2048]{0:T(1024)}, u32[]{:S(2)}) copy-start(f32[2048]{0:T(1024)} %param.17) | copy-start | bytes 24580
  16.7 117.1 %all-reduce.8.cloned.1.call-start = ((), (), s32[]{:S(2)}) async-start(), calls=%async_computation | async-start | bytes 393216 | tf_op jit(solution)/shard_map/psum | solution.py:30
  56.4 2.4 copy-start
  113.8 156.1 %all-reduce.12.cloned.1.call-start = ((), (), s32[]{:S(2)}) async-start(), calls=%async_computation.2 | async-start | bytes 3538944 | tf_op jit(solution)/shard_map/psum | solution.py:29
  117.7 22.2 %slice-start = ((s8[5505024]{0:T(1024)(128)(4,1)}), s8[1310720]{0:T(1024)(128)(4,1)S(1)}, s32[]{:S(2)}) async-start(s8[5505024]{0:T(1024)(128)(4,1)} %bitcast.41), calls=%async_computation.4 | async-start | bytes 2621440
  117.7 22.2 %copy-start.6 = (f32[2048]{0:T(1024)S(1)}, f32[2048]{0:T(1024)}, u32[]{:S(2)}) copy-start(f32[2048]{0:T(1024)} %param.16) | copy-start | bytes 24580
  133.8 6.1 %slice-start.4 = ((f32[4,168,2048]{2,1,0:T(8,128)}), f32[4,120,2048]{2,1,0:T(8,128)S(1)}, s32[]{:S(2)}) async-start(f32[4,168,2048]{2,1,0:T(8,128)} %copy-done), calls=%async_computation.8 | async-start | bytes 7864320 | tf_op jit(solution)/shard_map/slice | solution.py:78
  135.8 4.1 %slice-start.1 = ((s8[5505024]{0:T(1024)(128)(4,1)}), s8[4194304]{0:T(1024)(128)(4,1)S(1)}, s32[]{:S(2)}) async-start(s8[5505024]{0:T(1024)(128)(4,1)} %bitcast.41), calls=%async_computation.5 | async-start | bytes 8388608
  139.9 22.1 %copy-start.1 = (f32[4,48,2048]{2,1,0:T(8,128)}, f32[4,48,2048]{2,1,0:T(8,128)S(1)}, u32[]{:S(2)}) copy-start(f32[4,48,2048]{2,1,0:T(8,128)S(1)} %get-tuple-element.15) | copy-start | bytes 4718596
  150.2 1.1 copy-start.2
  150.3 2.4 slice-start.2
  150.5 2.6 slice-start.3
  165.6 2.4 copy-start.3
  174.2 115.6 %all-reduce.10.cloned.1.call-start = ((), (), s32[]{:S(2)}) async-start(), calls=%async_computation.1 | async-start | bytes 393216 | tf_op jit(solution)/shard_map/psum | solution.py:30
Sparse Core Ops, SparseCore 0:
  16.8 96.9 all-reduce.13
  116.2 17.5 all-reduce.7
  174.3 95.5 all-reduce.11
  272.1 17.6 all-reduce.9
